TPU v7x, 256 devices: a whole 4x4x8 slice. The times are simulated.
256 devices in a mesh: row: 8 (over x, core), col: 32 (over y, z).
Axes of the slice: x: 4, y: 4, z: 8, core: 2. Of those that a mesh axis runs over, the one named last changes fastest.
Arguments:
- connectivity: int32 [4, 2097152], P(None, ('row', 'col')), may hold values from 0 to 3071
- gradients: float32 [9, 2097152], P(None, ('row', 'col')), may hold values from -4 to 4
- volumes: float32 [2097152], P(('row', 'col')), may hold values from 0.2 to 1
- live_blocks: int32 [256], P(('row', 'col')), may hold values from 1 to 8, as said below
- send_lists: int32 [4, 65536], P(None, ('row', 'col')), may hold values from 0 to 2047
- divergence: float32 [524288], P(('row', 'col')), may hold values from -6 to 6
- mass_shift: float32 [524288], P(('row', 'col')), may hold values from 0.5 to 4
- boundary_nodes: int32 [81920], P(('row', 'col')), may hold values from 0 to 2047
- surface_points: float32 [3, 81920], P(None, ('row', 'col')), may hold values from 0 to 1
- normal_cos: float32 [81920], P(('row', 'col')), may hold values from -1 to 1
- normal_angle: float32 [81920], P(('row', 'col')), may hold values from -3.140625 to 3.140625
- node_areas: float32 [81920], P(('row', 'col')), may hold values from 0.00036621094 to 0.0014648438
Outputs:
- potential: float32 [524288], P(('row', 'col'))
- dirichlet: float32 [8192], P(('row', 'col'))
Inputs may be any that keep to these rules, and one draw needn't show every extreme that they name: The first live_blocks[p] element blocks of partition p are live, the rest are padding; some partition has all 8 blocks live. `connectivity`: indices into the partition's extended node list. `send_lists`: indices of the partition's own nodes. `boundary_nodes`: indices of the partition's own nodes.
All inputs are finite; a program needn't handle non-finite values.
Results may differ from a plain program's by a relative error of at most 0.0024.
Values sent between devices are 32-bit elements; how exact they have to be, the bound alone decides.
No kernel may reach another device: no remote copies, remote signals or barrier semaphores. Data moves between devices by JAX's collectives and lax.ppermute only.
A program may use at most 64 MiB of HBM per device.

v0:
```python
import math
import jax
import jax.numpy as jnp
from jax import lax
from jax.sharding import PartitionSpec as P

TGT_DEV = 32
NBLK = 8
ITERS = 3
smoothing = 0.0001
inverse_four_pi = 1.0 / (4.0 * math.pi)


def with_halo(block, sides, width):
    for axis, dim in sides:
        count = lax.axis_size(axis)
        forward = [(i, i + 1) for i in range(count - 1)]
        backward = [(target, source) for source, target in forward]
        low = lax.ppermute(
            lax.slice_in_dim(block, block.shape[dim] - width, None, axis=dim), axis, forward
        )
        high = lax.ppermute(lax.slice_in_dim(block, 0, width, axis=dim), axis, backward)
        block = jnp.concatenate([low, block, high], axis=dim)
    return block


def pick_block(total, largest):
    for candidate in range(min(total, largest), 0, -1):
        if total % candidate == 0:
            return candidate
    return 1


def element_terms(extended, corners, gradients, volumes):
    corner_values = extended[corners]
    grad_zero = gradients[0:3]
    grad_one = gradients[3:6]
    grad_two = gradients[6:9]
    grad_three = -(grad_zero + grad_one + grad_two)
    field_grad = (
        grad_zero * corner_values[0]
        + grad_one * corner_values[1]
        + grad_two * corner_values[2]
        + grad_three * corner_values[3]
    )
    return (
        jnp.stack(
            [
                jnp.sum(gradient * field_grad, axis=0)
                for gradient in (grad_zero, grad_one, grad_two, grad_three)
            ]
        )
        * volumes
    )


def kernel_rows(targets, sources):
    delta_x = targets[0][:, None] - sources[0][None, :]
    delta_y = targets[1][:, None] - sources[1][None, :]
    delta_z = targets[2][:, None] - sources[2][None, :]
    radius_sq = delta_x * delta_x + delta_y * delta_y + delta_z * delta_z + smoothing
    inverse = lax.rsqrt(radius_sq)
    numerator = (
        delta_x * sources[3][None, :]
        + delta_y * sources[4][None, :]
        + delta_z * sources[5][None, :]
    )
    entries = (numerator * (inverse * inverse * inverse) * inverse_four_pi).astype(jnp.bfloat16)
    return jnp.dot(entries, sources[6].astype(jnp.bfloat16), preferred_element_type=jnp.float32)


def fetch_ghosts(values, send_lists):
    picked = values[send_lists]
    empty = jnp.zeros_like(picked[0])
    layout = jnp.stack(
        [
            jnp.stack([empty, picked[1], empty]),
            jnp.stack([picked[3], empty, picked[2]]),
            jnp.stack([empty, picked[0], empty]),
        ]
    )
    extended = with_halo(layout, (("row", 0), ("col", 1)), 1)
    return jnp.concatenate([extended[0, 2], extended[4, 2], extended[2, 0], extended[2, 4]])


def return_ghosts(ghost_terms):
    empty = jnp.zeros_like(ghost_terms[0])
    layout = jnp.stack(
        [
            jnp.stack([empty, ghost_terms[0], empty]),
            jnp.stack([ghost_terms[2], empty, ghost_terms[3]]),
            jnp.stack([empty, ghost_terms[1], empty]),
        ]
    )
    extended = with_halo(layout, (("row", 0), ("col", 1)), 1)
    return jnp.stack([extended[4, 2], extended[0, 2], extended[2, 4], extended[2, 0]])


def apply_operator(values, connectivity, gradients, volumes, live_blocks, send_lists, mass_shift):
    nodes = values.shape[0]
    extended = jnp.concatenate([values, fetch_ghosts(values, send_lists)])
    block_size = connectivity.shape[1] // NBLK

    def add_block(block_index, total):
        start = block_index * block_size
        corners = lax.dynamic_slice_in_dim(connectivity, start, block_size, 1)
        block_grads = lax.dynamic_slice_in_dim(gradients, start, block_size, 1)
        block_volumes = lax.dynamic_slice_in_dim(volumes, start, block_size, 0)
        return total.at[corners].add(element_terms(extended, corners, block_grads, block_volumes))

    assembled = lax.fori_loop(0, live_blocks[0], add_block, jnp.zeros(extended.shape, jnp.float32))
    owned = assembled[:nodes]
    ghost_terms = assembled[nodes:].reshape(4, -1)
    owned = owned.at[send_lists].add(return_ghosts(ghost_terms))
    return mass_shift * values + owned


def squares(residual):
    return lax.psum(jnp.sum(residual * residual), ("row", "col"))


def per_device(
    connectivity,
    gradients,
    volumes,
    live_blocks,
    send_lists,
    divergence,
    mass_shift,
    boundary_nodes,
    surface_points,
    normal_cos,
    normal_angle,
    node_areas,
):
    potential = jnp.zeros_like(divergence)
    residual = divergence
    direction = divergence
    norm_now = squares(residual)
    for iteration in range(ITERS):
        image = apply_operator(
            direction, connectivity, gradients, volumes, live_blocks, send_lists, mass_shift
        )
        alpha = norm_now / lax.psum(jnp.sum(direction * image), ("row", "col"))
        potential = potential + alpha * direction
        residual = residual - alpha * image
        norm_next = squares(residual)
        direction = residual + norm_next / norm_now * direction
        norm_now = norm_next
    traces = potential[boundary_nodes]
    trace_bf = traces.astype(jnp.bfloat16)
    sine = jnp.sqrt(1.0 - normal_cos * normal_cos)
    normals = jnp.stack([sine * jnp.cos(normal_angle), sine * jnp.sin(normal_angle), normal_cos])
    weighted = node_areas[None, :] * normals
    sources = jnp.concatenate(
        [surface_points, weighted, trace_bf.astype(jnp.float32)[None, :]], axis=0
    )
    target_points = surface_points[:, :TGT_DEV]
    target_traces = traces[:TGT_DEV]
    piece = lax.all_gather(sources, ("row", "col"), axis=1, tiled=True)
    width = piece.shape[1]
    step = pick_block(width, 4096)

    def add_part(part_index, running):
        columns = lax.dynamic_slice_in_dim(piece, part_index * step, step, 1)
        return running + kernel_rows(target_points, columns)

    far_field = lax.fori_loop(0, width // step, add_part, jnp.zeros((TGT_DEV,), jnp.float32))
    dirichlet = far_field - 0.5 * target_traces
    return (potential, dirichlet)


def solution(mesh):
    return jax.shard_map(
        per_device,
        mesh=mesh,
        in_specs=(
            P(None, ("row", "col")),
            P(None, ("row", "col")),
            P(("row", "col")),
            P(("row", "col")),
            P(None, ("row", "col")),
            P(("row", "col")),
            P(("row", "col")),
            P(("row", "col")),
            P(None, ("row", "col")),
            P(("row", "col")),
            P(("row", "col")),
            P(("row", "col")),
        ),
        out_specs=(P(("row", "col")), P(("row", "col"))),
        check_vma=False,
    )
```

profile of v0, /device:TPU:1, one launch (start us, length us, event | category | flops | bytes accessed | tf_op | source)
XLA Modules:
  0.0 1841.5 jit_solution(16345966479136023931)
XLA Ops:
  8.0 6.2 gather_fusion.3
  14.2 4.5 collective-permute-start
  18.7 1.9 collective-permute-start.1
  20.7 2.9 collective-permute-done.1
  23.6 3.5 collective-permute-start.2
  28.6 3.2 collective-permute-done.3
  31.8 144.6 %while.44 = (s32[]{:T(128)}, f32[3072]{0:T(1024)S(1)}, s32[]{:T(128)}, s32[4,8192]{1,0:T(4,128)S(1)}, f32[9,8192]{1,0:T(8,128)}, /*index=5*/f32[3072]{0:T(1024)S...) while((s32[]{:T(128)}, f32[3072]{0:T(1024)S(1)}, s32[]{:T(128)}, ...), condition=%wide.region_8.0_spmd, body=%wide.region_2.0_spmd.sunk | while | flops 88072 | bytes 393431 | solution.py:111
  32.5 23.0 %gather_fusion = f32[4096]{0:T(1024)S(1)} fusion(f32[3072]{0:T(1024)S(1)} %get-tuple-element.611, s32[4096]{0:T(1024)S(1)} %broadcast_clamp_fusion.7), kind=kCustom, calls=%fused_computation.clone.1 | custom fusion | bytes 49152 | tf_op jit(solution)/shard_map/while/body/gather | solution.py:35
  57.4 22.4 %scatter_fusion = f32[3072]{0:T(1024)S(1)} fusion(f32[3072]{0:T(1024)S(1)} %get-tuple-element.594, s32[4096]{0:T(1024)S(1)} %bitcast.295, f32[4096]{0:T(1024)S(1)} %bitcast.292), kind=kCustom, calls=%fused_computation.7.clone.1 | custom fusion | flops 4096 | bytes 65536 | tf_op jit(solution)/shard_map/while/body/scatter-add | solution.py:109
  80.4 23.0 %gather_fusion = f32[4096]{0:T(1024)S(1)} fusion(f32[3072]{0:T(1024)S(1)} %get-tuple-element.611, s32[4096]{0:T(1024)S(1)} %broadcast_clamp_fusion.7), kind=kCustom, calls=%fused_computation.clone.1 | custom fusion | bytes 49152 | tf_op jit(solution)/shard_map/while/body/gather | solution.py:35
  105.3 22.4 %scatter_fusion = f32[3072]{0:T(1024)S(1)} fusion(f32[3072]{0:T(1024)S(1)} %get-tuple-element.594, s32[4096]{0:T(1024)S(1)} %bitcast.295, f32[4096]{0:T(1024)S(1)} %bitcast.292), kind=kCustom, calls=%fused_computation.7.clone.1 | custom fusion | flops 4096 | bytes 65536 | tf_op jit(solution)/shard_map/while/body/scatter-add | solution.py:109
  128.4 23.0 %gather_fusion = f32[4096]{0:T(1024)S(1)} fusion(f32[3072]{0:T(1024)S(1)} %get-tuple-element.611, s32[4096]{0:T(1024)S(1)} %broadcast_clamp_fusion.7), kind=kCustom, calls=%fused_computation.clone.1 | custom fusion | bytes 49152 | tf_op jit(solution)/shard_map/while/body/gather | solution.py:35
  153.3 22.4 %scatter_fusion = f32[3072]{0:T(1024)S(1)} fusion(f32[3072]{0:T(1024)S(1)} %get-tuple-element.594, s32[4096]{0:T(1024)S(1)} %bitcast.295, f32[4096]{0:T(1024)S(1)} %bitcast.292), kind=kCustom, calls=%fused_computation.7.clone.1 | custom fusion | flops 4096 | bytes 65536 | tf_op jit(solution)/shard_map/while/body/scatter-add | solution.py:109
  176.4 1.9 collective-permute-start.5
  178.3 48.7 %collective-permute-start.4 = (f32[1,3,256]{2,1,0:T(4,128)S(1)}, f32[1,3,256]{2,1,0:T(4,128)S(1)}, u32[]{:S(2)}, u32[]{:S(2)}) collective-permute-start(f32[1,3,256]{2,1,0:T(4,128)S(1)} %get-tuple-element.353), channel_id=1, source_target_pairs={{32,0},{64,32},{96,64},{128,96},{160,128},{192,160},{224,192},{33,... | collective-permute-start | bytes 9224 | tf_op jit(solution)/shard_map/ppermute | solution.py:22
  230.5 58.1 %collective-permute-done.6 = f32[5,1,256]{2,1,0:T(1,128)S(1)} collective-permute-done((f32[5,1,256]{2,1,0:T(1,128)S(1)}, f32[5,1,256]{2,1,0:T(1,128)S(1)}, u32[]{:S(2)}, u32[]{:S(2)}) %collective-permute-start.6) | collective-permute-done | bytes 5152 | tf_op jit(solution)/shard_map/ppermute | solution.py:22
  288.6 6.1 scatter_fusion.3
  295.3 218.7 %all-reduce = (f32[]{:T(128)}, f32[]{:T(128)}) all-reduce(f32[]{:T(128)} %get-tuple-element.227, f32[]{:T(128)} %get-tuple-element.226), channel_id=1, replica_groups=mesh['row'=8,'col'=32] {'row','col'}, use_global_device_ids=true, to_apply=%region_1.0 | all-reduce | flops 2 | bytes 16 | tf_op jit(solution)/shard_map/psum | solution.py:119
  516.0 72.5 %psum.44 = f32[]{:T(128)} all-reduce(f32[]{:T(128)} %get-tuple-element.284), channel_id=1, replica_groups=mesh['row'=8,'col'=32] {'row','col'}, use_global_device_ids=true, to_apply=%region_13.0 | all-reduce | flops 1 | bytes 8 | tf_op jit(solution)/shard_map/psum | solution.py:119
  589.9 6.2 gather_fusion.4
  596.1 3.3 collective-permute-start.8
  599.5 1.9 collective-permute-start.9
  601.5 2.9 collective-permute-done.9
  604.4 3.7 collective-permute-start.10
  609.5 3.0 collective-permute-done.11
  612.5 144.6 %while.45 = (s32[]{:T(128)}, f32[3072]{0:T(1024)S(1)}, s32[]{:T(128)}, s32[4,8192]{1,0:T(4,128)S(1)}, f32[9,8192]{1,0:T(8,128)}, /*index=5*/f32[3072]{0:T(1024)S...) while((s32[]{:T(128)}, f32[3072]{0:T(1024)S(1)}, s32[]{:T(128)}, ...), condition=%wide.region_20.0_spmd, body=%wide.region_14.0_spmd.sunk | while | flops 88072 | bytes 393431 | solution.py:111
  613.2 23.0 %gather_fusion.1 = f32[4096]{0:T(1024)S(1)} fusion(f32[3072]{0:T(1024)S(1)} %get-tuple-element.650, s32[4096]{0:T(1024)S(1)} %broadcast_clamp_fusion.8), kind=kCustom, calls=%fused_computation.1.clone.1 | custom fusion | bytes 49152 | tf_op jit(solution)/shard_map/while/body/gather | solution.py:35
  638.1 22.4 %scatter_fusion.1 = f32[3072]{0:T(1024)S(1)} fusion(f32[3072]{0:T(1024)S(1)} %get-tuple-element.633, s32[4096]{0:T(1024)S(1)} %bitcast.296, f32[4096]{0:T(1024)S(1)} %bitcast.293), kind=kCustom, calls=%fused_computation.8.clone.1 | custom fusion | flops 4096 | bytes 65536 | tf_op jit(solution)/shard_map/while/body/scatter-add | solution.py:109
  661.1 23.0 %gather_fusion.1 = f32[4096]{0:T(1024)S(1)} fusion(f32[3072]{0:T(1024)S(1)} %get-tuple-element.650, s32[4096]{0:T(1024)S(1)} %broadcast_clamp_fusion.8), kind=kCustom, calls=%fused_computation.1.clone.1 | custom fusion | bytes 49152 | tf_op jit(solution)/shard_map/while/body/gather | solution.py:35
  686.0 22.4 %scatter_fusion.1 = f32[3072]{0:T(1024)S(1)} fusion(f32[3072]{0:T(1024)S(1)} %get-tuple-element.633, s32[4096]{0:T(1024)S(1)} %bitcast.296, f32[4096]{0:T(1024)S(1)} %bitcast.293), kind=kCustom, calls=%fused_computation.8.clone.1 | custom fusion | flops 4096 | bytes 65536 | tf_op jit(solution)/shard_map/while/body/scatter-add | solution.py:109
  709.1 23.0 %gather_fusion.1 = f32[4096]{0:T(1024)S(1)} fusion(f32[3072]{0:T(1024)S(1)} %get-tuple-element.650, s32[4096]{0:T(1024)S(1)} %broadcast_clamp_fusion.8), kind=kCustom, calls=%fused_computation.1.clone.1 | custom fusion | bytes 49152 | tf_op jit(solution)/shard_map/while/body/gather | solution.py:35
  734.0 22.4 %scatter_fusion.1 = f32[3072]{0:T(1024)S(1)} fusion(f32[3072]{0:T(1024)S(1)} %get-tuple-element.633, s32[4096]{0:T(1024)S(1)} %bitcast.296, f32[4096]{0:T(1024)S(1)} %bitcast.293), kind=kCustom, calls=%fused_computation.8.clone.1 | custom fusion | flops 4096 | bytes 65536 | tf_op jit(solution)/shard_map/while/body/scatter-add | solution.py:109
  757.1 1.9 collective-permute-start.13
  759.0 48.9 %collective-permute-start.12 = (f32[1,3,256]{2,1,0:T(4,128)S(1)}, f32[1,3,256]{2,1,0:T(4,128)S(1)}, u32[]{:S(2)}, u32[]{:S(2)}) collective-permute-start(f32[1,3,256]{2,1,0:T(4,128)S(1)} %get-tuple-element.349), channel_id=1, source_target_pairs={{32,0},{64,32},{96,64},{128,96},{160,128},{192,160},{224,192},{33,... | collective-permute-start | bytes 9224 | tf_op jit(solution)/shard_map/ppermute | solution.py:22
  811.4 53.7 %collective-permute-done.14 = f32[5,1,256]{2,1,0:T(1,128)S(1)} collective-permute-done((f32[5,1,256]{2,1,0:T(1,128)S(1)}, f32[5,1,256]{2,1,0:T(1,128)S(1)}, u32[]{:S(2)}, u32[]{:S(2)}) %collective-permute-start.14) | collective-permute-done | bytes 5152 | tf_op jit(solution)/shard_map/ppermute | solution.py:22
  865.1 6.1 scatter_fusion.4
  871.8 216.6 %psum.45 = f32[]{:T(128)} all-reduce(f32[]{:T(128)} %multiply_reduce_fusion.14), channel_id=1, replica_groups=mesh['row'=8,'col'=32] {'row','col'}, use_global_device_ids=true, to_apply=%region_23.0 | all-reduce | flops 1 | bytes 8 | tf_op jit(solution)/shard_map/psum | solution.py:144
  1090.4 73.1 %psum.46 = f32[]{:T(128)} all-reduce(f32[]{:T(128)} %multiply_reduce_fusion.13), channel_id=1, replica_groups=mesh['row'=8,'col'=32] {'row','col'}, use_global_device_ids=true, to_apply=%region_25.0 | all-reduce | flops 1 | bytes 8 | tf_op jit(solution)/shard_map/psum | solution.py:119
  1164.8 6.2 gather_fusion.5
  1171.0 3.0 collective-permute-start.16
  1174.0 1.9 collective-permute-start.17
  1176.0 2.9 collective-permute-done.17
  1179.0 3.7 collective-permute-start.18
  1184.0 3.0 collective-permute-done.19
  1187.0 144.6 %while.46 = (s32[]{:T(128)}, f32[3072]{0:T(1024)S(1)}, s32[]{:T(128)}, s32[4,8192]{1,0:T(4,128)S(1)}, f32[9,8192]{1,0:T(8,128)}, /*index=5*/f32[3072]{0:T(1024)S...) while((s32[]{:T(128)}, f32[3072]{0:T(1024)S(1)}, s32[]{:T(128)}, ...), condition=%wide.region_32.0_spmd, body=%wide.region_26.0_spmd.sunk | while | flops 88072 | bytes 393431 | solution.py:111
  1187.7 23.0 %gather_fusion.2 = f32[4096]{0:T(1024)S(1)} fusion(f32[3072]{0:T(1024)S(1)} %get-tuple-element.689, s32[4096]{0:T(1024)S(1)} %broadcast_clamp_fusion.9), kind=kCustom, calls=%fused_computation.2.clone.1 | custom fusion | bytes 49152 | tf_op jit(solution)/shard_map/while/body/gather | solution.py:35
  1212.6 22.4 %scatter_fusion.2 = f32[3072]{0:T(1024)S(1)} fusion(f32[3072]{0:T(1024)S(1)} %get-tuple-element.672, s32[4096]{0:T(1024)S(1)} %bitcast.297, f32[4096]{0:T(1024)S(1)} %bitcast.294), kind=kCustom, calls=%fused_computation.9.clone.1 | custom fusion | flops 4096 | bytes 65536 | tf_op jit(solution)/shard_map/while/body/scatter-add | solution.py:109
  1235.7 23.0 %gather_fusion.2 = f32[4096]{0:T(1024)S(1)} fusion(f32[3072]{0:T(1024)S(1)} %get-tuple-element.689, s32[4096]{0:T(1024)S(1)} %broadcast_clamp_fusion.9), kind=kCustom, calls=%fused_computation.2.clone.1 | custom fusion | bytes 49152 | tf_op jit(solution)/shard_map/while/body/gather | solution.py:35
  1260.6 22.4 %scatter_fusion.2 = f32[3072]{0:T(1024)S(1)} fusion(f32[3072]{0:T(1024)S(1)} %get-tuple-element.672, s32[4096]{0:T(1024)S(1)} %bitcast.297, f32[4096]{0:T(1024)S(1)} %bitcast.294), kind=kCustom, calls=%fused_computation.9.clone.1 | custom fusion | flops 4096 | bytes 65536 | tf_op jit(solution)/shard_map/while/body/scatter-add | solution.py:109
  1283.7 23.0 %gather_fusion.2 = f32[4096]{0:T(1024)S(1)} fusion(f32[3072]{0:T(1024)S(1)} %get-tuple-element.689, s32[4096]{0:T(1024)S(1)} %broadcast_clamp_fusion.9), kind=kCustom, calls=%fused_computation.2.clone.1 | custom fusion | bytes 49152 | tf_op jit(solution)/shard_map/while/body/gather | solution.py:35
  1308.6 22.4 %scatter_fusion.2 = f32[3072]{0:T(1024)S(1)} fusion(f32[3072]{0:T(1024)S(1)} %get-tuple-element.672, s32[4096]{0:T(1024)S(1)} %bitcast.297, f32[4096]{0:T(1024)S(1)} %bitcast.294), kind=kCustom, calls=%fused_computation.9.clone.1 | custom fusion | flops 4096 | bytes 65536 | tf_op jit(solution)/shard_map/while/body/scatter-add | solution.py:109
  1331.6 1.9 collective-permute-start.21
  1333.6 48.9 %collective-permute-start.20 = (f32[1,3,256]{2,1,0:T(4,128)S(1)}, f32[1,3,256]{2,1,0:T(4,128)S(1)}, u32[]{:S(2)}, u32[]{:S(2)}) collective-permute-start(f32[1,3,256]{2,1,0:T(4,128)S(1)} %get-tuple-element.345), channel_id=1, source_target_pairs={{32,0},{64,32},{96,64},{128,96},{160,128},{192,160},{224,192},{33,... | collective-permute-start | bytes 9224 | tf_op jit(solution)/shard_map/ppermute | solution.py:22
  1385.9 53.7 %collective-permute-done.22 = f32[5,1,256]{2,1,0:T(1,128)S(1)} collective-permute-done((f32[5,1,256]{2,1,0:T(1,128)S(1)}, f32[5,1,256]{2,1,0:T(1,128)S(1)}, u32[]{:S(2)}, u32[]{:S(2)}) %collective-permute-start.22) | collective-permute-done | bytes 5152 | tf_op jit(solution)/shard_map/ppermute | solution.py:22
  1439.6 6.1 scatter_fusion.5
  1446.4 216.6 %psum.47 = f32[]{:T(128)} all-reduce(f32[]{:T(128)} %multiply_reduce_fusion.12), channel_id=1, replica_groups=mesh['row'=8,'col'=32] {'row','col'}, use_global_device_ids=true, to_apply=%region_35.0 | all-reduce | flops 1 | bytes 8 | tf_op jit(solution)/shard_map/psum | solution.py:144
  1664.3 2.2 gather_fusion.6
  1667.3 100.3 %all-gather.3.cloned.1.call-done = f32[256,320,7]{1,2,0:T(8,128)} async-done(((f32[1,320,7]{1,2,0:T(8,128)}), f32[256,320,7]{1,2,0:T(8,128)}) %all-gather.3.cloned.1.call-update) | async-done | bytes 2293776 | tf_op jit(solution)/shard_map/all_gather | solution.py:160
  1767.5 2.4 copy.16
  1770.0 2.8 reshape.207
  1772.8 61.3 %while.47 = (s32[]{:T(128)}, f32[32]{0:T(128)S(1)}, f32[3,32]{1,0:T(4,128)S(1)}, f32[7,81920]{1,0:T(8,128)}, s32[]{:T(128)}, /*index=5*/s32[]{:T(128)}, s32[]{:T...) while((s32[]{:T(128)}, f32[32]{0:T(128)S(1)}, f32[3,32]{1,0:T(4,128)S(1)}, ...), condition=%wide.region_37.0_spmd.clone, body=%wide.region_36.0_spmd.clone.sunk | while | flops 2752589 | bytes 312997 | solution.py:168
  1782.0 1.8 constant_dynamic-slice_fusion.2
  1794.4 1.8 constant_dynamic-slice_fusion.2
  1818.9 1.8 constant_dynamic-slice_fusion.2
  (296 shorter events, 91.9 us)
Async XLA Ops:
  7.2 0.8 copy-start
  7.2 24.6 %copy-start.2 = (s32[4,8192]{1,0:T(4,128)S(1)}, s32[4,8192]{1,0:T(4,128)}, u32[]{:S(2)}) copy-start(s32[4,8192]{1,0:T(4,128)} %param.20) | copy-start | bytes 393220
  7.2 1760.3 %all-gather.3.cloned.1.call-start = ((), (), s32[]{:S(2)}) async-start(), calls=%async_computation | async-start | bytes 3158016 | tf_op jit(solution)/shard_map/all_gather | solution.py:160
  14.2 6.4 collective-permute-start
  18.7 4.9 collective-permute-start.1
  23.6 4.9 collective-permute-start.2
  27.2 4.6 collective-permute-start.3
  31.7 195.3 %copy-start.3 = (f32[2048]{0:T(1024)S(1)}, f32[2048]{0:T(1024)}, u32[]{:S(2)}) copy-start(f32[2048]{0:T(1024)} %param.26) | copy-start | bytes 24580
  176.4 50.6 %collective-permute-start.5 = (f32[1,3,256]{2,1,0:T(4,128)S(1)}, f32[1,3,256]{2,1,0:T(4,128)S(1)}, u32[]{:S(2)}, u32[]{:S(2)}) collective-permute-start(f32[1,3,256]{2,1,0:T(4,128)S(1)} %get-tuple-element.354), channel_id=1, source_target_pairs={{0,32},{32,64},{64,96},{96,128},{128,160},{160,192},{192,224},{1,3... | collective-permute-start | bytes 9224 | tf_op jit(solution)/shard_map/ppermute | solution.py:19
  178.3 49.5 %collective-permute-start.4 = (f32[1,3,256]{2,1,0:T(4,128)S(1)}, f32[1,3,256]{2,1,0:T(4,128)S(1)}, u32[]{:S(2)}, u32[]{:S(2)}) collective-permute-start(f32[1,3,256]{2,1,0:T(4,128)S(1)} %get-tuple-element.353), channel_id=1, source_target_pairs={{32,0},{64,32},{96,64},{128,96},{160,128},{192,160},{224,192},{33,... | collective-permute-start | bytes 9224 | tf_op jit(solution)/shard_map/ppermute | solution.py:22
  227.8 2.6 collective-permute-start.7
  229.1 59.4 %collective-permute-start.6 = (f32[5,1,256]{2,1,0:T(1,128)S(1)}, f32[5,1,256]{2,1,0:T(1,128)S(1)}, u32[]{:S(2)}, u32[]{:S(2)}) collective-permute-start(f32[5,1,256]{2,1,0:T(1,128)S(1)} %get-tuple-element.315), channel_id=1, source_target_pairs={{1,0},{2,1},{3,2},{4,3},{5,4},{6,5},{7,6},{8,7},{9,8},{10,9},{11,1... | collective-permute-start | bytes 15368 | tf_op jit(solution)/shard_map/ppermute | solution.py:22
  294.7 304.7 %copy-start.5 = (f32[320]{0:T(512)S(1)}, f32[320]{0:T(512)}, u32[]{:S(2)}) copy-start(f32[320]{0:T(512)} %param.29) | copy-start | bytes 3844
  294.7 304.7 %copy-start.8 = (f32[320]{0:T(512)S(1)}, f32[320]{0:T(512)}, u32[]{:S(2)}) copy-start(f32[320]{0:T(512)} %param.30) | copy-start | bytes 3844
  596.1 5.3 collective-permute-start.8
  599.5 4.9 collective-permute-start.9
  604.4 5.0 collective-permute-start.10
  608.1 4.4 collective-permute-start.11
  757.1 50.8 %collective-permute-start.13 = (f32[1,3,256]{2,1,0:T(4,128)S(1)}, f32[1,3,256]{2,1,0:T(4,128)S(1)}, u32[]{:S(2)}, u32[]{:S(2)}) collective-permute-start(f32[1,3,256]{2,1,0:T(4,128)S(1)} %get-tuple-element.350), channel_id=1, source_target_pairs={{0,32},{32,64},{64,96},{96,128},{128,160},{160,192},{192,224},{1,3... | collective-permute-start | bytes 9224 | tf_op jit(solution)/shard_map/ppermute | solution.py:19
  759.0 49.7 %collective-permute-start.12 = (f32[1,3,256]{2,1,0:T(4,128)S(1)}, f32[1,3,256]{2,1,0:T(4,128)S(1)}, u32[]{:S(2)}, u32[]{:S(2)}) collective-permute-start(f32[1,3,256]{2,1,0:T(4,128)S(1)} %get-tuple-element.349), channel_id=1, source_target_pairs={{32,0},{64,32},{96,64},{128,96},{160,128},{192,160},{224,192},{33,... | collective-permute-start | bytes 9224 | tf_op jit(solution)/shard_map/ppermute | solution.py:22
  808.7 2.6 collective-permute-start.15
  810.0 55.0 %collective-permute-start.14 = (f32[5,1,256]{2,1,0:T(1,128)S(1)}, f32[5,1,256]{2,1,0:T(1,128)S(1)}, u32[]{:S(2)}, u32[]{:S(2)}) collective-permute-start(f32[5,1,256]{2,1,0:T(1,128)S(1)} %get-tuple-element.311), channel_id=1, source_target_pairs={{1,0},{2,1},{3,2},{4,3},{5,4},{6,5},{7,6},{8,7},{9,8},{10,9},{11,1... | collective-permute-start | bytes 15368 | tf_op jit(solution)/shard_map/ppermute | solution.py:22
  865.1 225.3 %copy-start.6 = (f32[320]{0:T(512)S(1)}, f32[320]{0:T(512)}, u32[]{:S(2)}) copy-start(f32[320]{0:T(512)} %param.31) | copy-start | bytes 3844
  871.2 302.8 %copy-start.7 = (s32[320]{0:T(512)S(1)}, s32[320]{0:T(512)}, u32[]{:S(2)}) copy-start(s32[320]{0:T(512)} %param.27) | copy-start | bytes 3844
  1171.0 5.0 collective-permute-start.16
  1174.0 4.9 collective-permute-start.17
  1179.0 5.0 collective-permute-start.18
  1182.6 4.4 collective-permute-start.19
  1331.6 50.8 %collective-permute-start.21 = (f32[1,3,256]{2,1,0:T(4,128)S(1)}, f32[1,3,256]{2,1,0:T(4,128)S(1)}, u32[]{:S(2)}, u32[]{:S(2)}) collective-permute-start(f32[1,3,256]{2,1,0:T(4,128)S(1)} %get-tuple-element.346), channel_id=1, source_target_pairs={{0,32},{32,64},{64,96},{96,128},{128,160},{160,192},{192,224},{1,3... | collective-permute-start | bytes 9224 | tf_op jit(solution)/shard_map/ppermute | solution.py:19
  1333.6 49.7 %collective-permute-start.20 = (f32[1,3,256]{2,1,0:T(4,128)S(1)}, f32[1,3,256]{2,1,0:T(4,128)S(1)}, u32[]{:S(2)}, u32[]{:S(2)}) collective-permute-start(f32[1,3,256]{2,1,0:T(4,128)S(1)} %get-tuple-element.345), channel_id=1, source_target_pairs={{32,0},{64,32},{96,64},{128,96},{160,128},{192,160},{224,192},{33,... | collective-permute-start | bytes 9224 | tf_op jit(solution)/shard_map/ppermute | solution.py:22
  1383.3 2.6 collective-permute-start.23
  1384.6 55.0 %collective-permute-start.22 = (f32[5,1,256]{2,1,0:T(1,128)S(1)}, f32[5,1,256]{2,1,0:T(1,128)S(1)}, u32[]{:S(2)}, u32[]{:S(2)}) collective-permute-start(f32[5,1,256]{2,1,0:T(1,128)S(1)} %get-tuple-element.307), channel_id=1, source_target_pairs={{1,0},{2,1},{3,2},{4,3},{5,4},{6,5},{7,6},{8,7},{9,8},{10,9},{11,1... | collective-permute-start | bytes 15368 | tf_op jit(solution)/shard_map/ppermute | solution.py:22
  1439.6 227.0 %copy-start.4 = (f32[3,320]{1,0:T(4,128)S(1)}, f32[3,320]{1,0:T(4,128)}, u32[]{:S(2)}) copy-start(f32[3,320]{1,0:T(4,128)} %param.28) | copy-start | bytes 11524
  1664.3 105.6 %copy-start.1 = (f32[2048]{0:T(1024)}, f32[2048]{0:T(1024)S(1)}, u32[]{:S(2)}) copy-start(f32[2048]{0:T(1024)S(1)} %multiply_add_fusion.3) | copy-start | bytes 24580
  1770.0 2.9 slice-start
Sparse Core Ops, SparseCore 0:
  1667.4 100.1 all-gather.2
where the time goes:
time: 1850 us; the launch traced here: 1840 us
  blocking collectives  798 us (43%)
  waiting for transfers between devices  286 us (15%)
  local copies, waits for them, and re-layouts  272 us (15%)
  other arithmetic  235 us (13%)
  starting transfers between devices  191 us (10%)
  matrix products  28.8 us (2%)
  between operations  21.8 us (1%)
    psum x2, blocking collectives, per_device(): alpha = norm_now / lax.psum(jnp.sum(direction * image), ('row', 'col'))  433 us
    psum x3, blocking collectives, squares(): return lax.psum(jnp.sum(residual * residual), ('row', 'col'))  364 us
    gather x9, local copies, waits for them, and re-layouts, element_terms(): corner_values = extended[corners]  207 us
    scatter-add x9, other arithmetic, add_block(): total.at[corners]  201 us
    ppermute x12, waiting for transfers between devices, with_halo(): lax.ppermute(lax.slice_in_dim(block, 0, width, axis=dim), axis, backward)  185 us
    ppermute x12, starting transfers between devices, with_halo(): lax.ppermute(lax.slice_in_dim(block, 0, width, axis=dim), axis, backward)  160 us
    all_gather x1, waiting for transfers between devices, per_device(): piece = lax.all_gather(sources, ('row', 'col'), axis=1, tiled=True)  100 us
  transfers between devices with their start and end apart: 25, of which 13 were waited for; matrix products, arithmetic and copies ran while one was open for 0% of the time, Pallas kernels for 0%

commit v1 on v0

--- a/solution.py
+++ b/solution.py
@@ -157,7 +157,10 @@
     )
     target_points = surface_points[:, :TGT_DEV]
     target_traces = traces[:TGT_DEV]
-    piece = lax.all_gather(sources, ("row", "col"), axis=1, tiled=True)
+    piece = jnp.concatenate(
+        lax.all_to_all(jnp.stack([sources] * lax.axis_size(("row", "col"))), ("row", "col"), 0, 0),
+        axis=1,
+    )
     width = piece.shape[1]
     step = pick_block(width, 4096)
 

time: 1850 us -> 1770 us (0.957)
  local copies, waits for them, and re-layouts: 272 us -> 247 us
  waiting for transfers between devices: 286 us -> 262 us
    all_gather x1 -> x0, waiting for transfers between devices: 100 us -> none  [per_device(): piece = lax.all_gather(sources, ('row', 'col'), axis=1, tiled=True)]
    all_to_all x0 -> x1, waiting for transfers between devices: none -> 76.4 us  [per_device(): lax.all_to_all(jnp.stack([sources] * lax.axis_size(('row', 'col'))), ('ro...]
    slice x20, local copies, waits for them, and re-layouts: 32.1 us -> 4.99 us  [kernel_rows(): delta_x = targets[0][:, None] - sources[0][None, :]]
where the time goes in v1:
time: 1770 us
  blocking collectives  798 us (45%)
  waiting for transfers between devices  262 us (15%)
  local copies, waits for them, and re-layouts  247 us (14%)
  other arithmetic  235 us (13%)
  starting transfers between devices  198 us (11%)
    psum x2, blocking collectives, per_device(): alpha = norm_now / lax.psum(jnp.sum(direction * image), ('row', 'col'))  433 us
    psum x3, blocking collectives, squares(): return lax.psum(jnp.sum(residual * residual), ('row', 'col'))  364 us
    gather x9, local copies, waits for them, and re-layouts, element_terms(): corner_values = extended[corners]  207 us
    scatter-add x9, other arithmetic, add_block(): total.at[corners]  201 us
    ppermute x12, waiting for transfers between devices, with_halo(): lax.ppermute(lax.slice_in_dim(block, 0, width, axis=dim), axis, backward)  185 us
    ppermute x12, starting transfers between devices, with_halo(): lax.ppermute(lax.slice_in_dim(block, 0, width, axis=dim), axis, backward)  160 us
    all_to_all x1, waiting for transfers between devices, per_device(): lax.all_to_all(jnp.stack([sources] * lax.axis_size(('row', 'col'))), ('ro...  76.4 us
  transfers between devices with their start and end apart: 25, of which 13 were waited for; matrix products, arithmetic and copies ran while one was open for 0% of the time, Pallas kernels for 0%

profile of v1, /device:TPU:1, one launch (start us, length us, event | category | flops | bytes accessed | tf_op | source)
XLA Modules:
  0.0 1766.7 jit_solution(1143407738781331305)
XLA Ops:
  1.4 6.2 gather_fusion.3
  7.6 4.5 collective-permute-start
  12.1 1.9 collective-permute-start.1
  14.1 2.9 collective-permute-done.1
  17.1 3.5 collective-permute-start.2
  22.0 3.2 collective-permute-done.3
  25.2 144.6 %while.44 = (s32[]{:T(128)}, f32[3072]{0:T(1024)S(1)}, s32[]{:T(128)}, s32[4,8192]{1,0:T(4,128)S(1)}, f32[9,8192]{1,0:T(8,128)}, /*index=5*/f32[3072]{0:T(1024)S...) while((s32[]{:T(128)}, f32[3072]{0:T(1024)S(1)}, s32[]{:T(128)}, ...), condition=%wide.region_8.0_spmd, body=%wide.region_2.0_spmd.sunk | while | flops 88072 | bytes 393431 | solution.py:111
  25.9 23.0 %gather_fusion = f32[4096]{0:T(1024)S(1)} fusion(f32[3072]{0:T(1024)S(1)} %get-tuple-element.611, s32[4096]{0:T(1024)S(1)} %broadcast_clamp_fusion.7), kind=kCustom, calls=%fused_computation.clone.1 | custom fusion | bytes 49152 | tf_op jit(solution)/shard_map/while/body/gather | solution.py:35
  50.8 22.4 %scatter_fusion = f32[3072]{0:T(1024)S(1)} fusion(f32[3072]{0:T(1024)S(1)} %get-tuple-element.594, s32[4096]{0:T(1024)S(1)} %bitcast.289, f32[4096]{0:T(1024)S(1)} %bitcast.286), kind=kCustom, calls=%fused_computation.7.clone.1 | custom fusion | flops 4096 | bytes 65536 | tf_op jit(solution)/shard_map/while/body/scatter-add | solution.py:109
  73.9 23.0 %gather_fusion = f32[4096]{0:T(1024)S(1)} fusion(f32[3072]{0:T(1024)S(1)} %get-tuple-element.611, s32[4096]{0:T(1024)S(1)} %broadcast_clamp_fusion.7), kind=kCustom, calls=%fused_computation.clone.1 | custom fusion | bytes 49152 | tf_op jit(solution)/shard_map/while/body/gather | solution.py:35
  98.8 22.4 %scatter_fusion = f32[3072]{0:T(1024)S(1)} fusion(f32[3072]{0:T(1024)S(1)} %get-tuple-element.594, s32[4096]{0:T(1024)S(1)} %bitcast.289, f32[4096]{0:T(1024)S(1)} %bitcast.286), kind=kCustom, calls=%fused_computation.7.clone.1 | custom fusion | flops 4096 | bytes 65536 | tf_op jit(solution)/shard_map/while/body/scatter-add | solution.py:109
  121.8 23.0 %gather_fusion = f32[4096]{0:T(1024)S(1)} fusion(f32[3072]{0:T(1024)S(1)} %get-tuple-element.611, s32[4096]{0:T(1024)S(1)} %broadcast_clamp_fusion.7), kind=kCustom, calls=%fused_computation.clone.1 | custom fusion | bytes 49152 | tf_op jit(solution)/shard_map/while/body/gather | solution.py:35
  146.7 22.4 %scatter_fusion = f32[3072]{0:T(1024)S(1)} fusion(f32[3072]{0:T(1024)S(1)} %get-tuple-element.594, s32[4096]{0:T(1024)S(1)} %bitcast.289, f32[4096]{0:T(1024)S(1)} %bitcast.286), kind=kCustom, calls=%fused_computation.7.clone.1 | custom fusion | flops 4096 | bytes 65536 | tf_op jit(solution)/shard_map/while/body/scatter-add | solution.py:109
  169.8 1.9 collective-permute-start.5
  171.7 48.7 %collective-permute-start.4 = (f32[1,3,256]{2,1,0:T(4,128)S(1)}, f32[1,3,256]{2,1,0:T(4,128)S(1)}, u32[]{:S(2)}, u32[]{:S(2)}) collective-permute-start(f32[1,3,256]{2,1,0:T(4,128)S(1)} %get-tuple-element.353), channel_id=1, source_target_pairs={{32,0},{64,32},{96,64},{128,96},{160,128},{192,160},{224,192},{33,... | collective-permute-start | bytes 9224 | tf_op jit(solution)/shard_map/ppermute | solution.py:22
  222.5 1.3 collective-permute-start.6
  223.9 58.1 %collective-permute-done.6 = f32[5,1,256]{2,1,0:T(1,128)S(1)} collective-permute-done((f32[5,1,256]{2,1,0:T(1,128)S(1)}, f32[5,1,256]{2,1,0:T(1,128)S(1)}, u32[]{:S(2)}, u32[]{:S(2)}) %collective-permute-start.6) | collective-permute-done | bytes 5152 | tf_op jit(solution)/shard_map/ppermute | solution.py:22
  282.0 6.1 scatter_fusion.3
  288.7 218.7 %all-reduce = (f32[]{:T(128)}, f32[]{:T(128)}) all-reduce(f32[]{:T(128)} %get-tuple-element.227, f32[]{:T(128)} %get-tuple-element.226), channel_id=1, replica_groups=mesh['row'=8,'col'=32] {'row','col'}, use_global_device_ids=true, to_apply=%region_1.0 | all-reduce | flops 2 | bytes 16 | tf_op jit(solution)/shard_map/psum | solution.py:119
  509.4 72.5 %psum.44 = f32[]{:T(128)} all-reduce(f32[]{:T(128)} %get-tuple-element.284), channel_id=1, replica_groups=mesh['row'=8,'col'=32] {'row','col'}, use_global_device_ids=true, to_apply=%region_13.0 | all-reduce | flops 1 | bytes 8 | tf_op jit(solution)/shard_map/psum | solution.py:119
  583.3 6.2 gather_fusion.4
  589.5 3.3 collective-permute-start.8
  592.9 1.9 collective-permute-start.9
  594.9 2.9 collective-permute-done.9
  597.8 3.7 collective-permute-start.10
  602.9 3.0 collective-permute-done.11
  605.9 144.6 %while.45 = (s32[]{:T(128)}, f32[3072]{0:T(1024)S(1)}, s32[]{:T(128)}, s32[4,8192]{1,0:T(4,128)S(1)}, f32[9,8192]{1,0:T(8,128)}, /*index=5*/f32[3072]{0:T(1024)S...) while((s32[]{:T(128)}, f32[3072]{0:T(1024)S(1)}, s32[]{:T(128)}, ...), condition=%wide.region_20.0_spmd, body=%wide.region_14.0_spmd.sunk | while | flops 88072 | bytes 393431 | solution.py:111
  606.6 23.0 %gather_fusion.1 = f32[4096]{0:T(1024)S(1)} fusion(f32[3072]{0:T(1024)S(1)} %get-tuple-element.650, s32[4096]{0:T(1024)S(1)} %broadcast_clamp_fusion.8), kind=kCustom, calls=%fused_computation.1.clone.1 | custom fusion | bytes 49152 | tf_op jit(solution)/shard_map/while/body/gather | solution.py:35
  631.5 22.4 %scatter_fusion.1 = f32[3072]{0:T(1024)S(1)} fusion(f32[3072]{0:T(1024)S(1)} %get-tuple-element.633, s32[4096]{0:T(1024)S(1)} %bitcast.290, f32[4096]{0:T(1024)S(1)} %bitcast.287), kind=kCustom, calls=%fused_computation.8.clone.1 | custom fusion | flops 4096 | bytes 65536 | tf_op jit(solution)/shard_map/while/body/scatter-add | solution.py:109
  654.6 23.0 %gather_fusion.1 = f32[4096]{0:T(1024)S(1)} fusion(f32[3072]{0:T(1024)S(1)} %get-tuple-element.650, s32[4096]{0:T(1024)S(1)} %broadcast_clamp_fusion.8), kind=kCustom, calls=%fused_computation.1.clone.1 | custom fusion | bytes 49152 | tf_op jit(solution)/shard_map/while/body/gather | solution.py:35
  679.5 22.4 %scatter_fusion.1 = f32[3072]{0:T(1024)S(1)} fusion(f32[3072]{0:T(1024)S(1)} %get-tuple-element.633, s32[4096]{0:T(1024)S(1)} %bitcast.290, f32[4096]{0:T(1024)S(1)} %bitcast.287), kind=kCustom, calls=%fused_computation.8.clone.1 | custom fusion | flops 4096 | bytes 65536 | tf_op jit(solution)/shard_map/while/body/scatter-add | solution.py:109
  702.5 23.0 %gather_fusion.1 = f32[4096]{0:T(1024)S(1)} fusion(f32[3072]{0:T(1024)S(1)} %get-tuple-element.650, s32[4096]{0:T(1024)S(1)} %broadcast_clamp_fusion.8), kind=kCustom, calls=%fused_computation.1.clone.1 | custom fusion | bytes 49152 | tf_op jit(solution)/shard_map/while/body/gather | solution.py:35
  727.4 22.4 %scatter_fusion.1 = f32[3072]{0:T(1024)S(1)} fusion(f32[3072]{0:T(1024)S(1)} %get-tuple-element.633, s32[4096]{0:T(1024)S(1)} %bitcast.290, f32[4096]{0:T(1024)S(1)} %bitcast.287), kind=kCustom, calls=%fused_computation.8.clone.1 | custom fusion | flops 4096 | bytes 65536 | tf_op jit(solution)/shard_map/while/body/scatter-add | solution.py:109
  750.5 1.9 collective-permute-start.13
  752.4 48.9 %collective-permute-start.12 = (f32[1,3,256]{2,1,0:T(4,128)S(1)}, f32[1,3,256]{2,1,0:T(4,128)S(1)}, u32[]{:S(2)}, u32[]{:S(2)}) collective-permute-start(f32[1,3,256]{2,1,0:T(4,128)S(1)} %get-tuple-element.349), channel_id=1, source_target_pairs={{32,0},{64,32},{96,64},{128,96},{160,128},{192,160},{224,192},{33,... | collective-permute-start | bytes 9224 | tf_op jit(solution)/shard_map/ppermute | solution.py:22
  804.8 53.7 %collective-permute-done.14 = f32[5,1,256]{2,1,0:T(1,128)S(1)} collective-permute-done((f32[5,1,256]{2,1,0:T(1,128)S(1)}, f32[5,1,256]{2,1,0:T(1,128)S(1)}, u32[]{:S(2)}, u32[]{:S(2)}) %collective-permute-start.14) | collective-permute-done | bytes 5152 | tf_op jit(solution)/shard_map/ppermute | solution.py:22
  858.5 6.1 scatter_fusion.4
  865.2 216.6 %psum.45 = f32[]{:T(128)} all-reduce(f32[]{:T(128)} %multiply_reduce_fusion.14), channel_id=1, replica_groups=mesh['row'=8,'col'=32] {'row','col'}, use_global_device_ids=true, to_apply=%region_23.0 | all-reduce | flops 1 | bytes 8 | tf_op jit(solution)/shard_map/psum | solution.py:144
  1083.8 73.1 %psum.46 = f32[]{:T(128)} all-reduce(f32[]{:T(128)} %multiply_reduce_fusion.13), channel_id=1, replica_groups=mesh['row'=8,'col'=32] {'row','col'}, use_global_device_ids=true, to_apply=%region_25.0 | all-reduce | flops 1 | bytes 8 | tf_op jit(solution)/shard_map/psum | solution.py:119
  1158.2 6.2 gather_fusion.5
  1164.4 3.0 collective-permute-start.16
  1167.4 1.9 collective-permute-start.17
  1169.4 2.9 collective-permute-done.17
  1172.4 3.7 collective-permute-start.18
  1177.5 3.0 collective-permute-done.19
  1180.5 144.6 %while.46 = (s32[]{:T(128)}, f32[3072]{0:T(1024)S(1)}, s32[]{:T(128)}, s32[4,8192]{1,0:T(4,128)S(1)}, f32[9,8192]{1,0:T(8,128)}, /*index=5*/f32[3072]{0:T(1024)S...) while((s32[]{:T(128)}, f32[3072]{0:T(1024)S(1)}, s32[]{:T(128)}, ...), condition=%wide.region_32.0_spmd, body=%wide.region_26.0_spmd.sunk | while | flops 88072 | bytes 393431 | solution.py:111
  1181.2 23.0 %gather_fusion.2 = f32[4096]{0:T(1024)S(1)} fusion(f32[3072]{0:T(1024)S(1)} %get-tuple-element.689, s32[4096]{0:T(1024)S(1)} %broadcast_clamp_fusion.9), kind=kCustom, calls=%fused_computation.2.clone.1 | custom fusion | bytes 49152 | tf_op jit(solution)/shard_map/while/body/gather | solution.py:35
  1206.1 22.4 %scatter_fusion.2 = f32[3072]{0:T(1024)S(1)} fusion(f32[3072]{0:T(1024)S(1)} %get-tuple-element.672, s32[4096]{0:T(1024)S(1)} %bitcast.291, f32[4096]{0:T(1024)S(1)} %bitcast.288), kind=kCustom, calls=%fused_computation.9.clone.1 | custom fusion | flops 4096 | bytes 65536 | tf_op jit(solution)/shard_map/while/body/scatter-add | solution.py:109
  1229.1 23.0 %gather_fusion.2 = f32[4096]{0:T(1024)S(1)} fusion(f32[3072]{0:T(1024)S(1)} %get-tuple-element.689, s32[4096]{0:T(1024)S(1)} %broadcast_clamp_fusion.9), kind=kCustom, calls=%fused_computation.2.clone.1 | custom fusion | bytes 49152 | tf_op jit(solution)/shard_map/while/body/gather | solution.py:35
  1254.0 22.4 %scatter_fusion.2 = f32[3072]{0:T(1024)S(1)} fusion(f32[3072]{0:T(1024)S(1)} %get-tuple-element.672, s32[4096]{0:T(1024)S(1)} %bitcast.291, f32[4096]{0:T(1024)S(1)} %bitcast.288), kind=kCustom, calls=%fused_computation.9.clone.1 | custom fusion | flops 4096 | bytes 65536 | tf_op jit(solution)/shard_map/while/body/scatter-add | solution.py:109
  1277.1 23.0 %gather_fusion.2 = f32[4096]{0:T(1024)S(1)} fusion(f32[3072]{0:T(1024)S(1)} %get-tuple-element.689, s32[4096]{0:T(1024)S(1)} %broadcast_clamp_fusion.9), kind=kCustom, calls=%fused_computation.2.clone.1 | custom fusion | bytes 49152 | tf_op jit(solution)/shard_map/while/body/gather | solution.py:35
  1302.0 22.4 %scatter_fusion.2 = f32[3072]{0:T(1024)S(1)} fusion(f32[3072]{0:T(1024)S(1)} %get-tuple-element.672, s32[4096]{0:T(1024)S(1)} %bitcast.291, f32[4096]{0:T(1024)S(1)} %bitcast.288), kind=kCustom, calls=%fused_computation.9.clone.1 | custom fusion | flops 4096 | bytes 65536 | tf_op jit(solution)/shard_map/while/body/scatter-add | solution.py:109
  1325.1 1.9 collective-permute-start.21
  1327.0 48.9 %collective-permute-start.20 = (f32[1,3,256]{2,1,0:T(4,128)S(1)}, f32[1,3,256]{2,1,0:T(4,128)S(1)}, u32[]{:S(2)}, u32[]{:S(2)}) collective-permute-start(f32[1,3,256]{2,1,0:T(4,128)S(1)} %get-tuple-element.345), channel_id=1, source_target_pairs={{32,0},{64,32},{96,64},{128,96},{160,128},{192,160},{224,192},{33,... | collective-permute-start | bytes 9224 | tf_op jit(solution)/shard_map/ppermute | solution.py:22
  1379.4 53.7 %collective-permute-done.22 = f32[5,1,256]{2,1,0:T(1,128)S(1)} collective-permute-done((f32[5,1,256]{2,1,0:T(1,128)S(1)}, f32[5,1,256]{2,1,0:T(1,128)S(1)}, u32[]{:S(2)}, u32[]{:S(2)}) %collective-permute-start.22) | collective-permute-done | bytes 5152 | tf_op jit(solution)/shard_map/ppermute | solution.py:22
  1433.1 6.1 scatter_fusion.5
  1439.8 216.6 %psum.47 = f32[]{:T(128)} all-reduce(f32[]{:T(128)} %multiply_reduce_fusion.12), channel_id=1, replica_groups=mesh['row'=8,'col'=32] {'row','col'}, use_global_device_ids=true, to_apply=%region_35.0 | all-reduce | flops 1 | bytes 8 | tf_op jit(solution)/shard_map/psum | solution.py:144
  1657.8 2.2 gather_fusion.6
  1660.1 1.9 stack.176
  1661.9 6.4 all-to-all-start
  1668.4 76.4 %all-to-all-done = f32[256,7,320]{2,1,0:T(8,128)S(1)} async-done(((f32[256,7,320]{2,1,0:T(8,128)}), f32[256,7,320]{2,1,0:T(8,128)S(1)}, u32[]{:S(2)}, u32[]{:S(2)}) %all-to-all-start) | async-done | bytes 2293792 | tf_op jit(solution)/shard_map/all_to_all | solution.py:161
  1744.8 2.1 copy.14
  1746.9 3.1 reshape.49
  1750.0 16.1 while.47
  (296 shorter events, 50.1 us)
Async XLA Ops:
  0.6 0.8 copy-start
  0.6 24.5 %copy-start.2 = (s32[4,8192]{1,0:T(4,128)S(1)}, s32[4,8192]{1,0:T(4,128)}, u32[]{:S(2)}) copy-start(s32[4,8192]{1,0:T(4,128)} %param.20) | copy-start | bytes 393220
  7.6 6.4 collective-permute-start
  12.1 4.9 collective-permute-start.1
  17.1 4.9 collective-permute-start.2
  20.6 4.6 collective-permute-start.3
  25.2 195.3 %copy-start.3 = (f32[2048]{0:T(1024)S(1)}, f32[2048]{0:T(1024)}, u32[]{:S(2)}) copy-start(f32[2048]{0:T(1024)} %param.26) | copy-start | bytes 24580
  169.8 50.6 %collective-permute-start.5 = (f32[1,3,256]{2,1,0:T(4,128)S(1)}, f32[1,3,256]{2,1,0:T(4,128)S(1)}, u32[]{:S(2)}, u32[]{:S(2)}) collective-permute-start(f32[1,3,256]{2,1,0:T(4,128)S(1)} %get-tuple-element.354), channel_id=1, source_target_pairs={{0,32},{32,64},{64,96},{96,128},{128,160},{160,192},{192,224},{1,3... | collective-permute-start | bytes 9224 | tf_op jit(solution)/shard_map/ppermute | solution.py:19
  171.7 49.5 %collective-permute-start.4 = (f32[1,3,256]{2,1,0:T(4,128)S(1)}, f32[1,3,256]{2,1,0:T(4,128)S(1)}, u32[]{:S(2)}, u32[]{:S(2)}) collective-permute-start(f32[1,3,256]{2,1,0:T(4,128)S(1)} %get-tuple-element.353), channel_id=1, source_target_pairs={{32,0},{64,32},{96,64},{128,96},{160,128},{192,160},{224,192},{33,... | collective-permute-start | bytes 9224 | tf_op jit(solution)/shard_map/ppermute | solution.py:22
  221.3 2.6 collective-permute-start.7
  222.5 59.4 %collective-permute-start.6 = (f32[5,1,256]{2,1,0:T(1,128)S(1)}, f32[5,1,256]{2,1,0:T(1,128)S(1)}, u32[]{:S(2)}, u32[]{:S(2)}) collective-permute-start(f32[5,1,256]{2,1,0:T(1,128)S(1)} %get-tuple-element.315), channel_id=1, source_target_pairs={{1,0},{2,1},{3,2},{4,3},{5,4},{6,5},{7,6},{8,7},{9,8},{10,9},{11,1... | collective-permute-start | bytes 15368 | tf_op jit(solution)/shard_map/ppermute | solution.py:22
  288.1 304.7 %copy-start.5 = (f32[320]{0:T(512)S(1)}, f32[320]{0:T(512)}, u32[]{:S(2)}) copy-start(f32[320]{0:T(512)} %param.29) | copy-start | bytes 3844
  288.1 304.7 %copy-start.8 = (f32[320]{0:T(512)S(1)}, f32[320]{0:T(512)}, u32[]{:S(2)}) copy-start(f32[320]{0:T(512)} %param.30) | copy-start | bytes 3844
  589.5 5.3 collective-permute-start.8
  592.9 4.9 collective-permute-start.9
  597.8 5.0 collective-permute-start.10
  601.5 4.4 collective-permute-start.11
  750.5 50.8 %collective-permute-start.13 = (f32[1,3,256]{2,1,0:T(4,128)S(1)}, f32[1,3,256]{2,1,0:T(4,128)S(1)}, u32[]{:S(2)}, u32[]{:S(2)}) collective-permute-start(f32[1,3,256]{2,1,0:T(4,128)S(1)} %get-tuple-element.350), channel_id=1, source_target_pairs={{0,32},{32,64},{64,96},{96,128},{128,160},{160,192},{192,224},{1,3... | collective-permute-start | bytes 9224 | tf_op jit(solution)/shard_map/ppermute | solution.py:19
  752.4 49.7 %collective-permute-start.12 = (f32[1,3,256]{2,1,0:T(4,128)S(1)}, f32[1,3,256]{2,1,0:T(4,128)S(1)}, u32[]{:S(2)}, u32[]{:S(2)}) collective-permute-start(f32[1,3,256]{2,1,0:T(4,128)S(1)} %get-tuple-element.349), channel_id=1, source_target_pairs={{32,0},{64,32},{96,64},{128,96},{160,128},{192,160},{224,192},{33,... | collective-permute-start | bytes 9224 | tf_op jit(solution)/shard_map/ppermute | solution.py:22
  802.1 2.6 collective-permute-start.15
  803.4 55.0 %collective-permute-start.14 = (f32[5,1,256]{2,1,0:T(1,128)S(1)}, f32[5,1,256]{2,1,0:T(1,128)S(1)}, u32[]{:S(2)}, u32[]{:S(2)}) collective-permute-start(f32[5,1,256]{2,1,0:T(1,128)S(1)} %get-tuple-element.311), channel_id=1, source_target_pairs={{1,0},{2,1},{3,2},{4,3},{5,4},{6,5},{7,6},{8,7},{9,8},{10,9},{11,1... | collective-permute-start | bytes 15368 | tf_op jit(solution)/shard_map/ppermute | solution.py:22
  858.5 225.3 %copy-start.6 = (f32[320]{0:T(512)S(1)}, f32[320]{0:T(512)}, u32[]{:S(2)}) copy-start(f32[320]{0:T(512)} %param.31) | copy-start | bytes 3844
  864.6 302.8 %copy-start.7 = (s32[320]{0:T(512)S(1)}, s32[320]{0:T(512)}, u32[]{:S(2)}) copy-start(s32[320]{0:T(512)} %param.27) | copy-start | bytes 3844
  1164.4 5.0 collective-permute-start.16
  1167.4 4.9 collective-permute-start.17
  1172.4 5.0 collective-permute-start.18
  1176.1 4.4 collective-permute-start.19
  1325.1 50.8 %collective-permute-start.21 = (f32[1,3,256]{2,1,0:T(4,128)S(1)}, f32[1,3,256]{2,1,0:T(4,128)S(1)}, u32[]{:S(2)}, u32[]{:S(2)}) collective-permute-start(f32[1,3,256]{2,1,0:T(4,128)S(1)} %get-tuple-element.346), channel_id=1, source_target_pairs={{0,32},{32,64},{64,96},{96,128},{128,160},{160,192},{192,224},{1,3... | collective-permute-start | bytes 9224 | tf_op jit(solution)/shard_map/ppermute | solution.py:19
  1327.0 49.7 %collective-permute-start.20 = (f32[1,3,256]{2,1,0:T(4,128)S(1)}, f32[1,3,256]{2,1,0:T(4,128)S(1)}, u32[]{:S(2)}, u32[]{:S(2)}) collective-permute-start(f32[1,3,256]{2,1,0:T(4,128)S(1)} %get-tuple-element.345), channel_id=1, source_target_pairs={{32,0},{64,32},{96,64},{128,96},{160,128},{192,160},{224,192},{33,... | collective-permute-start | bytes 9224 | tf_op jit(solution)/shard_map/ppermute | solution.py:22
  1376.7 2.6 collective-permute-start.23
  1378.0 55.0 %collective-permute-start.22 = (f32[5,1,256]{2,1,0:T(1,128)S(1)}, f32[5,1,256]{2,1,0:T(1,128)S(1)}, u32[]{:S(2)}, u32[]{:S(2)}) collective-permute-start(f32[5,1,256]{2,1,0:T(1,128)S(1)} %get-tuple-element.307), channel_id=1, source_target_pairs={{1,0},{2,1},{3,2},{4,3},{5,4},{6,5},{7,6},{8,7},{9,8},{10,9},{11,1... | collective-permute-start | bytes 15368 | tf_op jit(solution)/shard_map/ppermute | solution.py:22
  1433.1 227.0 %copy-start.4 = (f32[3,320]{1,0:T(4,128)S(1)}, f32[3,320]{1,0:T(4,128)}, u32[]{:S(2)}) copy-start(f32[3,320]{1,0:T(4,128)} %param.28) | copy-start | bytes 11524
  1657.8 4.2 copy-start.1
  1661.9 82.9 %all-to-all-start = ((f32[256,7,320]{2,1,0:T(8,128)}), f32[256,7,320]{2,1,0:T(8,128)S(1)}, u32[]{:S(2)}, u32[]{:S(2)}) async-start(f32[256,7,320]{2,1,0:T(8,128)} %stack.176), calls=%async_computation | async-start | bytes 6291456 | tf_op jit(solution)/shard_map/all_to_all | solution.py:161
  1746.9 3.1 slice-start
